TPU v7x, 32 devices: a whole 2x2x4 slice. The times are simulated.
32 devices in a mesh: kf: 8 (over z, y), kc: 4 (over x, core).
Axes of the slice: x: 2, y: 2, z: 4, core: 2. Of those that a mesh axis runs over, the one named last changes fastest.
Arguments:
- kernel_coarse: bfloat16 [256, 256], P('kf'), may hold values from -6 to 6
- coefficients: bfloat16 [128, 256], P(('kf', 'kc')), may hold values from -1.5 to 1.5
- nearest: int32 [128], replicated, may hold values from 0 to 15
Outputs:
- kernel_fine: bfloat16 [2048, 2048], P('kf', 'kc')
All inputs are finite; a program needn't handle non-finite values.
Results may differ from a plain program's by a relative error of at most 0.0049.
Values may be sent and summed in bfloat16 or wider, within the bound.
A program may use at most 64 MiB of HBM per device.

v0:
```python
import jax
import jax.numpy as jnp
from jax import lax
from jax.sharding import PartitionSpec as P

P_SIZE = 16


def rotate(kernel_rows, coef_block):
    point_count = coef_block.shape[0]
    pair_count = coef_block.shape[1]
    shaped = kernel_rows.reshape(kernel_rows.shape[0], point_count, pair_count)
    turned = jnp.einsum("ckn,kan->cka", shaped, coef_block, preferred_element_type=jnp.float32)
    return turned.astype(jnp.bfloat16).reshape(kernel_rows.shape[0], point_count * pair_count)


def shards(kernel_coarse, coefficients, nearest):
    pair_count = P_SIZE
    total_rows = kernel_coarse.shape[1]
    fine_total = nearest.shape[0]
    slab_size = fine_total // lax.axis_size("kf")
    kc_count = lax.axis_size("kc")
    part_index = lax.axis_index("kc")
    offsets = jnp.arange(pair_count, dtype=jnp.int32)
    coef_whole = lax.all_gather(coefficients, ("kf", "kc"), axis=0, tiled=True).reshape(
        fine_total, pair_count, pair_count
    )
    share_size = slab_size // kc_count
    grouped = nearest.reshape(lax.axis_size("kf"), kc_count, share_size)
    chosen = lax.dynamic_index_in_dim(grouped, part_index, 1, keepdims=False)
    columns = (chosen.reshape(-1)[:, None] * pair_count + offsets[None, :]).reshape(-1)
    outgoing = jnp.take(kernel_coarse, columns, axis=1)
    received = lax.all_to_all(outgoing, "kf", split_axis=1, concat_axis=0, tiled=True)
    own_coef = coefficients.reshape(share_size, pair_count, pair_count)
    turned = rotate(received, own_coef)
    rotated = lax.all_gather(turned, "kc", axis=1, tiled=True)
    col_total = fine_total // kc_count
    col_coarse = lax.dynamic_slice_in_dim(nearest, part_index * col_total, col_total)
    coef_cols = lax.dynamic_slice_in_dim(coef_whole, part_index * col_total, col_total, 0)
    stacked = rotated.reshape(total_rows // pair_count, pair_count, rotated.shape[1])
    picked = jnp.take(stacked, col_coarse, axis=0)
    result = jnp.einsum("jnr,jbn->rjb", picked, coef_cols, preferred_element_type=jnp.float32)
    return result.reshape(result.shape[0], col_total * pair_count).astype(jnp.bfloat16)


def solution(mesh):
    in_specs = (P("kf", None), P(("kf", "kc"), None), P())
    out_specs = P("kf", "kc")
    return jax.shard_map(shards, mesh=mesh, in_specs=in_specs, out_specs=out_specs, check_vma=False)
```

profile of v0, /device:TPU:0, one launch (start us, length us, event | category | flops | bytes accessed | tf_op | source)
XLA Modules:
  0.0 63.8 jit_solution(2334305354638408349)
XLA Ops:
  0.0 0.0 copy-start.2
  0.0 0.7 %copy-done.2 = s32[128]{0:T(128)S(1)} copy-done((s32[128]{0:T(128)S(1)}, s32[128]{0:T(128)}, u32[]{:S(2)}) %copy-start.2) | copy-done | bytes 536
  0.7 0.1 reshape.90
  0.8 0.5 broadcast.58
  1.3 0.7 %fusion.6 = (s32[8,4]{1,0:T(8,128)S(1)}, s32[8,1,4]{2,1,0:T(1,128)S(1)}) fusion(s32[]{:T(128)} %broadcast.58, s32[8,4,4]{2,1,0:T(4,128)S(1)} %reshape.90, s32[]{:T(128)S(6)} %select_n.41), kind=kLoop, calls=%fused_computation.20 | loop fusion | flops 32 | bytes 392 | tf_op jit(solution)/shard_map/mul | solution.py:31
  2.0 0.1 mul.23
  2.0 0.1 add.82
  2.1 0.1 add.83
  2.2 0.1 iota_add_fusion
  2.3 0.1 add.92
  2.4 0.0 copy-start
  2.4 0.1 add.85
  2.5 0.6 copy-done
  3.1 0.1 copy.17
  3.2 1.3 %gather_fusion = bf16[512,32]{1,0:T(8,128)(2,1)S(1)} fusion(bf16[32,256]{0,1:T(8,128)(2,1)S(1)} %copy.17, s32[1024]{0:T(1024)S(1)} %pad_clamp_fusion.1), kind=kCustom, calls=%fused_computation | custom fusion | bytes 67584 | tf_op jit(solution)/shard_map/jit(_take)/gather | solution.py:32
  4.6 0.1 copy.18
  4.7 0.7 %reshape.124 = bf16[8,2,1024]{2,1,0:T(2,128)(2,1)} reshape(bf16[8,32,64]{2,1,0:T(8,128)(2,1)S(1)} %fusion.7) | data formatting | bytes 65536
  5.4 7.3 %all-to-all-start = ((bf16[8,2,1024]{2,1,0:T(2,128)(2,1)}), bf16[8,2,1024]{2,1,0:T(2,128)(2,1)S(1)}, u32[]{:S(2)}, u32[]{:S(2)}) async-start(bf16[8,2,1024]{2,1,0:T(2,128)(2,1)} %reshape.124), calls=%async_computation | async-start | bytes 65536 | tf_op jit(solution)/shard_map/all_to_all | solution.py:33
  12.8 0.0 copy-start.1
  12.8 0.1 compare_and_fusion.1
  12.8 0.6 copy-done.1
  13.4 0.1 reshape.92
  13.5 42.1 %all-gather = bf16[32,4,256]{2,1,0:T(4,128)(2,1)S(1)} all-gather(bf16[1,4,256]{2,1,0:T(4,128)(2,1)S(1)} %bitcast.28), channel_id=1, replica_groups=mesh['kf'=8,'kc'=4] {'kf','kc'}, dimensions={0}, use_global_device_ids=true | all-gather | bytes 67584 | tf_op jit(solution)/shard_map/all_gather | solution.py:25
  55.6 0.4 reshape.89
  56.0 0.0 all-to-all-done
  56.0 0.1 reshape.125
  56.1 0.1 copy.19
  56.3 0.1 reshape.91
  56.4 0.1 convolution_convert_fusion.1
  56.5 5.4 %all_gather.7 = bf16[256,256]{0,1:T(8,128)(2,1)S(1)} all-gather(bf16[256,64]{0,1:T(8,128)(2,1)S(1)} %bitcast.26), channel_id=1, replica_groups=mesh['kf'=8,'kc'=4] {'kc'}, dimensions={1}, use_global_device_ids=true | all-gather | bytes 163840 | tf_op jit(solution)/shard_map/all_gather | solution.py:36
  61.9 0.1 copy.20
  62.1 0.6 gather_fusion.1
  62.6 0.3 convolution_convert_fusion
  62.9 0.8 %copy.21 = bf16[256,512]{1,0:T(8,128)(2,1)} copy(bf16[256,512]{0,1:T(8,128)(2,1)S(1)} %bitcast.24) | data formatting | bytes 524288 | tf_op jit(solution)/shard_map/convert_element_type | solution.py:43
  (7 shorter events, 0.1 us)
Async XLA Ops:
  0.0 0.7 %copy-start.2 = (s32[128]{0:T(128)S(1)}, s32[128]{0:T(128)}, u32[]{:S(2)}) copy-start(s32[128]{0:T(128)} %param.5) | copy-start | bytes 1540
  2.4 0.7 %copy-start = (bf16[32,256]{1,0:T(8,128)(2,1)S(1)}, bf16[32,256]{1,0:T(8,128)(2,1)}, u32[]{:S(2)}) copy-start(bf16[32,256]{1,0:T(8,128)(2,1)} %param.3) | copy-start | bytes 49156
  5.4 50.6 %all-to-all-start = ((bf16[8,2,1024]{2,1,0:T(2,128)(2,1)}), bf16[8,2,1024]{2,1,0:T(2,128)(2,1)S(1)}, u32[]{:S(2)}, u32[]{:S(2)}) async-start(bf16[8,2,1024]{2,1,0:T(2,128)(2,1)} %reshape.124), calls=%async_computation | async-start | bytes 65536 | tf_op jit(solution)/shard_map/all_to_all | solution.py:33
  12.8 0.7 %copy-start.1 = (bf16[4,256]{1,0:T(4,128)(2,1)S(1)}, bf16[4,256]{1,0:T(4,128)(2,1)}, u32[]{:S(2)}) copy-start(bf16[4,256]{1,0:T(4,128)(2,1)} %param.4) | copy-start | bytes 6148
where the time goes:
time: 64.1 us; the launch traced here: 63.8 us
  blocking collectives  47.5 us (74%)
  local copies, waits for them, and re-layouts  7.54 us (12%)
  starting transfers between devices  7.31 us (11%)
  other arithmetic  0.86 us (1%)
    all_gather x1, blocking collectives, shards(): lax.all_gather(coefficients, ('kf', 'kc'), axis=0, tiled=True)  42.1 us
    all_to_all x1, starting transfers between devices, shards(): lax.all_to_all(outgoing, 'kf', split_axis=1, concat_axis=0, tiled=True)  7.31 us
    all_gather x1, blocking collectives, shards(): rotated = lax.all_gather(turned, 'kc', axis=1, tiled=True)  5.41 us
    unnamed x9, local copies, waits for them, and re-layouts  2.83 us
    gather x2, local copies, waits for them, and re-layouts, shards(): outgoing = jnp.take(kernel_coarse, columns, axis=1)  1.45 us
  transfers between devices with their start and end apart: 1, of which 0 were waited for; matrix products, arithmetic and copies ran while one was open for 1% of the time, Pallas kernels for 0%

commit v1 on v0

--- a/solution.py
+++ b/solution.py
@@ -33,7 +33,12 @@
     received = lax.all_to_all(outgoing, "kf", split_axis=1, concat_axis=0, tiled=True)
     own_coef = coefficients.reshape(share_size, pair_count, pair_count)
     turned = rotate(received, own_coef)
-    rotated = lax.all_gather(turned, "kc", axis=1, tiled=True)
+    ring = [turned]
+    for hop in range(3):
+        ring.append(lax.ppermute(ring[-1], "kc", [(dev, (dev + 1) % 4) for dev in range(4)]))
+    rotated = jnp.roll(
+        jnp.concatenate(ring[::-1], axis=1), (lax.axis_index("kc") + 1) * ring[0].shape[1], axis=1
+    )
     col_total = fine_total // kc_count
     col_coarse = lax.dynamic_slice_in_dim(nearest, part_index * col_total, col_total)
     coef_cols = lax.dynamic_slice_in_dim(coef_whole, part_index * col_total, col_total, 0)

time: 64.1 us -> 68.4 us (1.067)
  waiting for transfers between devices: 0.01 us -> 13.2 us
  blocking collectives: 47.5 us -> 38.1 us
    ppermute x0 -> x3, waiting for transfers between devices: none -> 7.27 us  [shards(): lax.ppermute(ring[-1], 'kc', [(dev, (dev + 1) % 4) for dev in range(4)])]
    all_to_all x1, waiting for transfers between devices: 0.01 us -> 5.92 us  [shards(): lax.all_to_all(outgoing, 'kf', split_axis=1, concat_axis=0, tiled=True)]
    all_gather x1 -> x0, blocking collectives: 5.41 us -> none  [shards(): rotated = lax.all_gather(turned, 'kc', axis=1, tiled=True)]
    all_gather x1, blocking collectives: 42.1 us -> 38.1 us  [shards(): lax.all_gather(coefficients, ('kf', 'kc'), axis=0, tiled=True)]
  transfers between devices with their start and end apart: 1 -> 4, of which waited for: 0 -> 3; matrix products, arithmetic and copies ran while one was open for 1% -> 1% of each run, Pallas kernels for 0% -> 0%
where the time goes in v1:
time: 68.4 us; the launch traced here: 68 us
  blocking collectives  38.1 us (56%)
  waiting for transfers between devices  13.2 us (19%)
  local copies, waits for them, and re-layouts  7.97 us (12%)
  starting transfers between devices  7.37 us (11%)
  other arithmetic  0.86 us (1%)
    all_gather x1, blocking collectives, shards(): lax.all_gather(coefficients, ('kf', 'kc'), axis=0, tiled=True)  38.1 us
    all_to_all x1, starting transfers between devices, shards(): lax.all_to_all(outgoing, 'kf', split_axis=1, concat_axis=0, tiled=True)  7.31 us
    ppermute x3, waiting for transfers between devices, shards(): lax.ppermute(ring[-1], 'kc', [(dev, (dev + 1) % 4) for dev in range(4)])  7.27 us
    all_to_all x1, waiting for transfers between devices, shards(): lax.all_to_all(outgoing, 'kf', split_axis=1, concat_axis=0, tiled=True)  5.92 us
    unnamed x9, local copies, waits for them, and re-layouts  2.92 us
    gather x2, local copies, waits for them, and re-layouts, shards(): outgoing = jnp.take(kernel_coarse, columns, axis=1)  1.45 us
  transfers between devices with their start and end apart: 4, of which 3 were waited for; matrix products, arithmetic and copies ran while one was open for 1% of the time, Pallas kernels for 0%

profile of v1, /device:TPU:0, one launch (start us, length us, event | category | flops | bytes accessed | tf_op | source)
XLA Modules:
  0.0 68.0 jit_solution(12442896667675240025)
XLA Ops:
  0.0 0.0 copy-start.2
  0.0 0.7 copy-done.2
  0.7 0.1 reshape.90
  0.8 0.5 broadcast.59
  1.3 0.7 fusion.6
  2.0 0.1 mul.26
  2.0 0.1 add.95
  2.1 0.1 add.96
  2.2 0.1 iota_add_fusion
  2.3 0.1 add.105
  2.4 0.0 copy-start
  2.4 0.1 add.98
  2.5 0.6 copy-done
  3.1 0.1 copy.19
  3.2 1.3 %gather_fusion = bf16[512,32]{1,0:T(8,128)(2,1)S(1)} fusion(bf16[32,256]{0,1:T(8,128)(2,1)S(1)} %copy.19, s32[1024]{0:T(1024)S(1)} %pad_clamp_fusion.1), kind=kCustom, calls=%fused_computation | custom fusion | bytes 67584 | tf_op jit(solution)/shard_map/jit(_take)/gather | solution.py:32
  4.6 0.1 copy.20
  4.7 0.7 %reshape.124 = bf16[8,2,1024]{2,1,0:T(2,128)(2,1)} reshape(bf16[8,32,64]{2,1,0:T(8,128)(2,1)S(1)} %fusion.7) | data formatting | bytes 65536
  5.4 7.3 %all-to-all-start = ((bf16[8,2,1024]{2,1,0:T(2,128)(2,1)}), bf16[8,2,1024]{2,1,0:T(2,128)(2,1)S(1)}, u32[]{:S(2)}, u32[]{:S(2)}) async-start(bf16[8,2,1024]{2,1,0:T(2,128)(2,1)} %reshape.124), calls=%async_computation | async-start | bytes 65536 | tf_op jit(solution)/shard_map/all_to_all | solution.py:33
  12.8 0.0 copy-start.1
  12.8 0.7 copy-done.1
  13.4 0.1 reshape.92
  13.5 5.9 %all-to-all-done = bf16[8,2,1024]{2,1,0:T(2,128)(2,1)S(1)} async-done(((bf16[8,2,1024]{2,1,0:T(2,128)(2,1)}), bf16[8,2,1024]{2,1,0:T(2,128)(2,1)S(1)}, u32[]{:S(2)}, u32[]{:S(2)}) %all-to-all-start) | async-done | bytes 32800 | tf_op jit(solution)/shard_map/all_to_all | solution.py:33
  19.4 0.1 reshape.125
  19.6 0.1 copy.21
  19.7 0.1 reshape.91
  19.8 0.1 convolution_convert_fusion.1
  20.0 0.1 copy.22
  20.1 0.1 collective-permute-start
  20.1 0.1 compare_and_fusion.1
  20.2 3.6 %collective-permute-done = bf16[256,64]{1,0:T(8,128)(2,1)S(1)} collective-permute-done((bf16[256,64]{1,0:T(8,128)(2,1)S(1)}, bf16[256,64]{1,0:T(8,128)(2,1)S(1)}, u32[]{:S(2)}, u32[]{:S(2)}) %collective-permute-start) | collective-permute-done | bytes 32800 | tf_op jit(solution)/shard_map/ppermute | solution.py:38
  23.8 0.0 collective-permute-start.1
  23.8 3.7 %collective-permute-done.1 = bf16[256,64]{1,0:T(8,128)(2,1)S(1)} collective-permute-done((bf16[256,64]{1,0:T(8,128)(2,1)S(1)}, bf16[256,64]{1,0:T(8,128)(2,1)S(1)}, u32[]{:S(2)}, u32[]{:S(2)}) %collective-permute-start.1) | collective-permute-done | bytes 32800 | tf_op jit(solution)/shard_map/ppermute | solution.py:38
  27.5 0.0 collective-permute-start.2
  27.5 38.1 %all-gather = bf16[32,4,256]{2,1,0:T(4,128)(2,1)S(1)} all-gather(bf16[1,4,256]{2,1,0:T(4,128)(2,1)S(1)} %bitcast.28), channel_id=1, replica_groups=mesh['kf'=8,'kc'=4] {'kf','kc'}, dimensions={0}, use_global_device_ids=true | all-gather | bytes 67584 | tf_op jit(solution)/shard_map/all_gather | solution.py:25
  65.6 0.4 reshape.89
  66.0 0.0 collective-permute-done.2
  66.0 0.2 concatenate.6
  66.2 0.1 constant_dynamic-slice_fusion
  66.3 0.6 gather_fusion.1
  66.9 0.3 convolution_convert_fusion
  67.2 0.8 %copy.25 = bf16[256,512]{1,0:T(8,128)(2,1)} copy(bf16[256,512]{0,1:T(8,128)(2,1)S(1)} %bitcast.24) | data formatting | bytes 524288 | tf_op jit(solution)/shard_map/convert_element_type | solution.py:48
  (7 shorter events, 0.1 us)
Async XLA Ops:
  0.0 0.7 copy-start.2
  2.4 0.7 %copy-start = (bf16[32,256]{1,0:T(8,128)(2,1)S(1)}, bf16[32,256]{1,0:T(8,128)(2,1)}, u32[]{:S(2)}) copy-start(bf16[32,256]{1,0:T(8,128)(2,1)} %param.3) | copy-start | bytes 49156
  5.4 14.0 %all-to-all-start = ((bf16[8,2,1024]{2,1,0:T(2,128)(2,1)}), bf16[8,2,1024]{2,1,0:T(2,128)(2,1)S(1)}, u32[]{:S(2)}, u32[]{:S(2)}) async-start(bf16[8,2,1024]{2,1,0:T(2,128)(2,1)} %reshape.124), calls=%async_computation | async-start | bytes 65536 | tf_op jit(solution)/shard_map/all_to_all | solution.py:33
  12.8 0.7 %copy-start.1 = (bf16[4,256]{1,0:T(4,128)(2,1)S(1)}, bf16[4,256]{1,0:T(4,128)(2,1)}, u32[]{:S(2)}) copy-start(bf16[4,256]{1,0:T(4,128)(2,1)} %param.4) | copy-start | bytes 6148
  20.1 3.7 %collective-permute-start = (bf16[256,64]{1,0:T(8,128)(2,1)S(1)}, bf16[256,64]{1,0:T(8,128)(2,1)S(1)}, u32[]{:S(2)}, u32[]{:S(2)}) collective-permute-start(bf16[256,64]{1,0:T(8,128)(2,1)S(1)} %copy.22), channel_id=1, source_target_pairs={{0,1},{1,2},{2,3},{3,0},{4,5},{5,6},{6,7},{7,4},{8,9},{9,10},{10,1... | collective-permute-start | bytes 98312 | tf_op jit(solution)/shard_map/ppermute | solution.py:38
  23.8 3.7 %collective-permute-start.1 = (bf16[256,64]{1,0:T(8,128)(2,1)S(1)}, bf16[256,64]{1,0:T(8,128)(2,1)S(1)}, u32[]{:S(2)}, u32[]{:S(2)}) collective-permute-start(bf16[256,64]{1,0:T(8,128)(2,1)S(1)} %collective-permute-done), channel_id=1, source_target_pairs={{0,1},{1,2},{2,3},{3,0},{4,5},{5,6},{6,7},{7,4},{8,9},{9,10},{10,1... | collective-permute-start | bytes 98312 | tf_op jit(solution)/shard_map/ppermute | solution.py:38
  27.5 38.5 %collective-permute-start.2 = (bf16[256,64]{1,0:T(8,128)(2,1)S(1)}, bf16[256,64]{1,0:T(8,128)(2,1)S(1)}, u32[]{:S(2)}, u32[]{:S(2)}) collective-permute-start(bf16[256,64]{1,0:T(8,128)(2,1)S(1)} %collective-permute-done.1), channel_id=1, source_target_pairs={{0,1},{1,2},{2,3},{3,0},{4,5},{5,6},{6,7},{7,4},{8,9},{9,10},{10,1... | collective-permute-start | bytes 98312 | tf_op jit(solution)/shard_map/ppermute | solution.py:38
